TPU v7x, 32 devices: a whole 2x2x4 slice. The times are simulated.
32 devices in a mesh: parts: 2 (over y), space: 8 (over z, x), tm: 2 (over core).
Axes of the slice: x: 2, y: 2, z: 4, core: 2. Of those that a mesh axis runs over, the one named last changes fastest.
Arguments:
- eigvecs: bfloat16 [4, 2, 256, 3, 1728], P(('parts', 'tm'), None, None, None, 'space'), parts along dimension 0, may hold values from -1.25 to 1.25
- links: bfloat16 [4, 3, 3, 3, 2, 1728], P(('parts', 'tm'), None, None, None, None, 'space'), parts along dimension 0, may hold values from -2.5 to 2.5
- dirs: int32 [3], replicated, may hold values from 0 to 2, each once
- peram: bfloat16 [4, 2, 1024, 1024], P(('parts', 'tm'), None, 'space'), parts along dimension 0, may hold values from -0.25 to 0.25
Outputs:
- meson_blocks: bfloat16 [4, 3, 2, 1024, 1024], P(('parts', 'tm'), None, None, 'space'), parts along dimension 0
There are 2 independent parts, one for each index of `parts`. A program takes and returns all parts, laid end to end along the dimension named above; an argument that names none is the same for every part. Nothing has to cross between parts.
All inputs are finite; a program needn't handle non-finite values.
Results may differ from a plain program's by a relative error of at most 0.0061.
Values may be sent and summed in bfloat16 or wider, within the bound.
No kernel may reach another device: no remote copies, remote signals or barrier semaphores. Data moves between devices by JAX's collectives and lax.ppermute only.
A program may use at most 64 MiB of HBM per device.

v0:
```python
import functools

import jax
import jax.numpy as jnp
from jax import lax
from jax.experimental import pallas as pl
from jax.experimental.pallas import tpu as pltpu
from jax.sharding import PartitionSpec as P


SPIN = 4
LX = 9
LZ = 24
F32 = jnp.float32
BF16 = jnp.bfloat16
VMEM = pl.BlockSpec(memory_space=pltpu.VMEM)
ANY = pl.BlockSpec(memory_space=pl.ANY)
HBM = pl.BlockSpec(memory_space=pltpu.HBM)
VMEM_BYTES = 67_043_328
PARAMS = pltpu.CompilerParams(vmem_limit_bytes=12 * 1024 * 1024)


def half_rows(sites):
    return 8 * ((sites + 15) // 16)


def padded(count):
    return 8 * ((count + 7) // 8)


def identity(size):
    rows = lax.broadcasted_iota(jnp.int32, (size, size), 0)
    cols = lax.broadcasted_iota(jnp.int32, (size, size), 1)
    return jnp.where(rows == cols, 1.0, 0.0).astype(BF16)


def dot(left, right, left_dim, right_dim):
    return lax.dot_general(
        left, right, (((left_dim,), (right_dim,)), ((), ())), preferred_element_type=F32
    )


def adjoint_product(columns, base, vec):
    real_rows, imag_rows = [], []
    for out in range(3):
        real_sum = imag_sum = None
        for inner in range(3):
            at = base + (inner * 3 + out) * 2
            link_real = columns[:, at : at + 1]
            link_imag = columns[:, at + 1 : at + 2]
            real = link_real * vec[inner] + link_imag * vec[3 + inner]
            imag = link_real * vec[3 + inner] - link_imag * vec[inner]
            real_sum = real if real_sum is None else real_sum + real
            imag_sum = imag if imag_sum is None else imag_sum + imag
        real_rows.append(real_sum)
        imag_rows.append(imag_sum)
    return real_rows + imag_rows


def packed_elemental(w_real, w_imag, v_real, v_imag):
    real = dot(w_real, v_real, 0, 0) + dot(w_imag, v_imag, 0, 0)
    imag = dot(w_real, v_imag, 0, 0) - dot(w_imag, v_real, 0, 0)
    return (real + imag) + jnp.transpose(imag - real)


def link_table(u_ref, first, last):
    return jnp.concatenate([u_ref[at].astype(F32) for at in range(first, last)], axis=0)


def prepare_kernel(sites, v_ref, u_ref, across_ref, along_ref, link_ref, sems, link_sem):
    half = half_rows(sites)
    overlap = 2 * half - sites
    vectors = v_ref.shape[1]
    parity = lax.rem(lax.axis_index("space"), 2)
    fetch = pltpu.make_async_copy(u_ref.at[pl.ds(9, 9)], link_ref, link_sem)
    fetch.start()
    copies = []
    for slot, (ref, upper) in enumerate(((across_ref, 1 - parity), (along_ref, parity))):
        for comp in range(6):
            first = pl.multiple_of(comp * sites + upper * (sites - half), 8)
            copy = pltpu.make_async_copy(
                v_ref.at[pl.ds(first, half)],
                ref.at[pl.ds(comp * half, half)],
                sems.at[slot, comp],
            )
            copy.start()
            copies.append(copy)
    fetch.wait()
    links = link_table(link_ref, 0, 9)
    rows = across_ref.shape[0] - 6 * half
    lower = links[:, :half]
    upper = links[:, sites - half :]
    lane = lax.broadcasted_iota(jnp.int32, upper.shape, 1)
    upper = jnp.where(lane < overlap, 0.0, upper)
    for ref, wanted in ((across_ref, 1 - parity), (along_ref, parity)):
        block = jnp.where(wanted == 1, upper, lower)
        block = jnp.concatenate([block, jnp.zeros((rows - block.shape[0], half), F32)], axis=0)
        block = jnp.concatenate([block, jnp.zeros((rows, vectors - half), F32)], axis=1)
        ref[pl.ds(6 * half, rows), :] = block.astype(BF16)
    for copy in copies:
        copy.wait()


def front_kernel(sites, v_ref, u_ref, o_ref, w_ref):
    planes = sites // LZ
    vectors = v_ref.shape[1]
    columns = dot(identity(sites), link_table(u_ref, 0, 27).astype(BF16), 1, 1)
    for plane in range(planes):
        slab, along = plane // LX, plane % LX
        start = plane * LZ
        vec = [v_ref[pl.ds(comp * sites + start, LZ), :].astype(F32) for comp in range(6)]
        here = columns[start : start + LZ, :]
        ahead = (slab * LX + (along + 1) % LX) * LZ
        for comp, value in enumerate(adjoint_product(here, 0, vec)):
            w_ref[0, pl.ds(comp * sites + ahead, LZ), :] = value
        for comp, value in enumerate(adjoint_product(here, 36, vec)):
            w_ref[1, pl.ds(comp * sites + start, LZ), :] = pltpu.roll(value, 1, 0)
    real = pl.ds(0, 3 * sites)
    imag = pl.ds(3 * sites, 3 * sites)
    for index in range(2):
        packed = packed_elemental(
            w_ref[index, real, :].astype(BF16),
            w_ref[index, imag, :].astype(BF16),
            v_ref[real, :],
            v_ref[imag, :],
        )
        o_ref[pl.ds(index * vectors, vectors), :] = packed.astype(BF16)


def rotated(half, field, w_ref):
    columns = dot(identity(half), field[6 * half :, :half], 1, 1)
    vec = [field[comp * half : (comp + 1) * half, :].astype(F32) for comp in range(6)]
    for comp, value in enumerate(adjoint_product(columns, 0, vec)):
        w_ref[pl.ds(comp * half, half), :] = value.astype(w_ref.dtype)


def early_kernel(half, own_ref, along_ref, w_ref):
    even = lax.rem(lax.axis_index("space"), 2) == 0
    rotated(half, jnp.where(even, own_ref[...], along_ref[...]), w_ref)


def late_kernel(half, early_ref, own_ref, across_ref, along_ref, flat_ref, *rest):
    chunks, w_ref, y_ref = rest[:-2], rest[-2], rest[-1]
    near = len(chunks)
    even = lax.rem(lax.axis_index("space"), 2) == 0
    rotated(half, across_ref[...], w_ref)
    real, imag = pl.ds(0, 3 * half), pl.ds(3 * half, 3 * half)
    packed = packed_elemental(
        early_ref[real, :], early_ref[imag, :], across_ref[real, :], across_ref[imag, :]
    ) + packed_elemental(
        w_ref[real, :].astype(BF16),
        w_ref[imag, :].astype(BF16),
        jnp.where(even, along_ref[real, :], own_ref[real, :]),
        jnp.where(even, along_ref[imag, :], own_ref[imag, :]),
    )
    y_ref[...] = packed.astype(BF16)
    place = lax.rem(lax.axis_index("space"), near)
    wide, narrow = flat_ref.shape[0] // near, y_ref.shape[0] // near
    for partner, chunk_ref in enumerate(chunks):
        chunk = jnp.bitwise_xor(place, partner)
        chunk_ref[pl.ds(0, wide), :] = flat_ref[pl.ds(pl.multiple_of(chunk * wide, wide), wide), :]
        chunk_ref[pl.ds(wide, narrow), :] = y_ref[
            pl.ds(pl.multiple_of(chunk * narrow, narrow), narrow), :
        ]


def spread(size):
    rows = lax.broadcasted_iota(jnp.int32, (SPIN * size, SPIN * size), 0)
    cols = lax.broadcasted_iota(jnp.int32, (SPIN * size, SPIN * size), 1)
    target = (rows % size) * SPIN + rows // size
    return jnp.where(cols == target, 1.0, 0.0).astype(BF16)


def spins_kernel(p_ref, minus_ref, plus_ref, s_ref):
    columns, wide = p_ref.shape[1], p_ref.shape[2]
    vectors = wide // SPIN
    block = 128
    table = spread(block)
    s_ref[...] = spread(s_ref.shape[0] // SPIN)
    for chunk in range(vectors // block):
        at = pl.ds(chunk * block * SPIN, block * SPIN)
        real = dot(p_ref[0, :, at], table, 1, 1)
        imag = dot(p_ref[1, :, at], table, 1, 1)
        less = (0.5 * (real - imag)).astype(BF16)
        more = (0.5 * (real + imag)).astype(BF16)
        to = pl.ds(chunk * block, block)
        for spin in range(SPIN):
            lanes = slice(spin * block, (spin + 1) * block)
            rows = pl.ds(2 * spin * columns, columns)
            below = pl.ds((2 * spin + 1) * columns, columns)
            minus_ref[rows, to] = less[:, lanes]
            minus_ref[below, to] = more[:, lanes]
            plus_ref[rows, to] = -more[:, lanes]
            plus_ref[below, to] = less[:, lanes]


def last_kernel(near, dirs_ref, *refs):
    chunks = refs[:near]
    minus_ref, plus_ref, s_ref, o_ref, flat_ref, y_ref, product_ref, whole_ref, sems = refs[near:]
    vectors = y_ref.shape[0]
    columns = o_ref.shape[2]
    block = s_ref.shape[0] // SPIN
    place = lax.rem(lax.axis_index("space"), near)
    wide, narrow = 2 * vectors // near, vectors // near
    for partner, chunk_ref in enumerate(chunks):
        chunk = jnp.bitwise_xor(place, partner)
        flat_ref[pl.ds(pl.multiple_of(chunk * wide, wide), wide), :] = chunk_ref[pl.ds(0, wide), :]
        y_ref[pl.ds(pl.multiple_of(chunk * narrow, narrow), narrow), :] = chunk_ref[
            pl.ds(wide, narrow), :
        ]
    copies = []

    def multiply(direction):
        if direction == 1:
            packed = y_ref[...]
        else:
            packed = flat_ref[pl.ds(direction // 2 * vectors, vectors), :]
        step = 4 * columns
        for first in range(0, 2 * SPIN * columns, step):
            rows = pl.ds(first, step)
            product_ref[direction, rows, :] = (
                dot(minus_ref[rows, :], packed, 1, 1) + dot(plus_ref[rows, :], packed, 1, 0)
            ).astype(BF16)

    def store(direction):
        to_place = jnp.where(dirs_ref[1] == direction, 1, jnp.where(dirs_ref[2] == direction, 2, 0))
        for chunk in range(vectors // block):
            piece = jnp.concatenate(
                [
                    product_ref[
                        direction,
                        pl.ds(2 * spin * columns, 2 * columns),
                        pl.ds(chunk * block, block),
                    ]
                    for spin in range(SPIN)
                ],
                axis=1,
            )
            apart = dot(piece, s_ref[...], 1, 0).astype(BF16)
            to = pl.ds(chunk * block * SPIN, block * SPIN)
            whole_ref[direction, 0, :, to] = apart[:columns]
            whole_ref[direction, 1, :, to] = apart[columns:]
            copy = pltpu.make_async_copy(
                whole_ref.at[direction, :, :, to],
                o_ref.at[to_place, :, :, to],
                sems.at[direction, chunk],
            )
            copy.start()
            copies.append(copy)

    multiply(0)
    multiply(2)
    store(0)
    multiply(1)
    store(2)
    store(1)
    for copy in copies:
        copy.wait()


def last_call(dirs, chunks, minus, plus, table, shape):
    near = len(chunks)
    vectors = chunks[0].shape[1]
    return pl.pallas_call(
        functools.partial(last_kernel, near),
        in_specs=[pl.BlockSpec(memory_space=pltpu.SMEM)] + [VMEM] * (near + 3),
        out_specs=HBM,
        out_shape=jax.ShapeDtypeStruct(shape, BF16),
        scratch_shapes=[
            pltpu.VMEM((2 * vectors, vectors), BF16),
            pltpu.VMEM((vectors, vectors), BF16),
            pltpu.VMEM((shape[0],) + minus.shape, BF16),
            pltpu.VMEM(shape, BF16),
            pltpu.SemaphoreType.DMA((shape[0], vectors * SPIN // table.shape[0])),
        ],
        cost_estimate=pl.CostEstimate(
            flops=2_400_000_000, bytes_accessed=3_000_000, transcendentals=0
        ),
        compiler_params=pltpu.CompilerParams(vmem_limit_bytes=12 * 1024 * 1024),
    )(dirs, *chunks, minus, plus, table)


def swap(block, ranks, distance):
    return lax.ppermute(block, "space", [(i, i ^ distance) for i in range(ranks)])


def sum_over_space(chunks, ranks):
    near = len(chunks)
    total = chunks[0].astype(F32)
    for partner in range(near - 1, 0, -1):
        total = total + swap(chunks[partner], ranks, partner).astype(F32)
    stride = near
    while stride < ranks:
        total = total + swap(total.astype(BF16), ranks, stride).astype(F32)
        stride *= 2
    whole = [total.astype(BF16)]
    for partner in range(1, near):
        whole.append(swap(whole[0], ranks, partner))
    return whole


def blocks(eigvecs, links, dirs, peram):
    ranks = lax.axis_size("space")
    vectors, sites = eigvecs.shape[2], eigvecs.shape[4]
    assert sites == LX * LZ and ranks % 2 == 0
    field = jnp.transpose(eigvecs[0], (0, 2, 3, 1)).reshape(6 * sites, vectors)
    link_rows = links[0].reshape(27, 2, sites)
    half = half_rows(sites)
    rows = 6 * half + padded(18)
    near = 4 if ranks % 4 == 0 else 2

    payload = pltpu.VMEM((rows, vectors), BF16)
    across, along = pl.pallas_call(
        functools.partial(prepare_kernel, sites),
        out_shape=(payload, payload),
        in_specs=[HBM, HBM],
        out_specs=(VMEM, VMEM),
        scratch_shapes=[
            pltpu.VMEM((9, 2, sites), BF16),
            pltpu.SemaphoreType.DMA((2, 6)),
            pltpu.SemaphoreType.DMA,
        ],
        compiler_params=pltpu.CompilerParams(vmem_limit_bytes=VMEM_BYTES - 4 * rows * vectors),
    )(field, link_rows)
    from_across = lax.ppermute(across, "space", [(i, i ^ 1) for i in range(ranks)])
    from_along = lax.ppermute(
        along,
        "space",
        [((i + 2) % ranks if i % 2 == 0 else (i - 2) % ranks, i) for i in range(ranks)],
    )
    partner = lax.ppermute(peram[0], "tm", [((i + 1) % 2, i) for i in range(2)])

    flat = pl.pallas_call(
        functools.partial(front_kernel, sites),
        out_shape=jax.ShapeDtypeStruct((2 * vectors, vectors), BF16),
        in_specs=[VMEM] * 2,
        out_specs=VMEM,
        scratch_shapes=[pltpu.VMEM((2, 6 * sites, vectors), F32)],
        cost_estimate=pl.CostEstimate(flops=700_000_000, bytes_accessed=8_000_000, transcendentals=0),
        compiler_params=PARAMS,
    )(field, link_rows)
    columns = partner.shape[1]
    minus, plus, table = pl.pallas_call(
        spins_kernel,
        out_shape=(
            jax.ShapeDtypeStruct((2 * SPIN * columns, vectors), BF16),
            jax.ShapeDtypeStruct((2 * SPIN * columns, vectors), BF16),
            jax.ShapeDtypeStruct((SPIN * 64, SPIN * 64), BF16),
        ),
        in_specs=[VMEM],
        out_specs=(VMEM, VMEM, VMEM),
        cost_estimate=pl.CostEstimate(flops=500_000_000, bytes_accessed=2_000_000, transcendentals=0),
        compiler_params=PARAMS,
    )(partner)
    early = pl.pallas_call(
        functools.partial(early_kernel, half),
        out_shape=jax.ShapeDtypeStruct((6 * half, vectors), BF16),
        in_specs=[VMEM] * 2,
        out_specs=VMEM,
        cost_estimate=pl.CostEstimate(
            flops=20_000_000, bytes_accessed=1_000_000, transcendentals=0
        ),
        compiler_params=PARAMS,
    )(along, from_along)
    chunks = pl.pallas_call(
        functools.partial(late_kernel, half),
        out_shape=[jax.ShapeDtypeStruct((3 * vectors // near, vectors), BF16)] * near,
        in_specs=[VMEM] * 5,
        out_specs=[VMEM] * near,
        scratch_shapes=[pltpu.VMEM((6 * half, vectors), F32), pltpu.VMEM((vectors, vectors), BF16)],
        cost_estimate=pl.CostEstimate(
            flops=400_000_000, bytes_accessed=2_000_000, transcendentals=0
        ),
        compiler_params=PARAMS,
    )(early, along, from_across, from_along, flat)
    chunks = sum_over_space(chunks, ranks)
    shape = (dirs.shape[0], 2, columns, SPIN * vectors)
    result = last_call(dirs, chunks, minus, plus, table, shape)
    return result[None]


def solution(mesh):
    placed = (
        P(("parts", "tm"), None, None, None, "space"),
        P(("parts", "tm"), None, None, None, None, "space"),
        P(),
        P(("parts", "tm"), None, "space", None),
    )
    return jax.shard_map(
        blocks,
        mesh=mesh,
        in_specs=placed,
        out_specs=P(("parts", "tm"), None, None, "space", None),
        check_vma=False,
    )
```

profile of v0, /device:TPU:0, one launch (start us, length us, event | category | flops | bytes accessed | tf_op | source)
XLA Modules:
  0.0 41.0 jit_solution(12931431485690873380)
XLA Ops:
  0.0 1.2 %shard_map.46 = (bf16[696,256]{1,0:T(8,128)(2,1)S(1)}, bf16[696,256]{1,0:T(8,128)(2,1)S(1)}) custom-call(bf16[1296,256]{1,0:T(8,128)(2,1)} %bitcast.8, bf16[27,2,216]{2,1,0:T(2,128)(2,1)} %bitcast.10), custom_call_target="tpu_custom_call" | custom-call | tf_op jit(solution)/shard_map/pallas_call | solution.py:313
  1.2 5.1 %collective-permute-start = (bf16[696,256]{1,0:T(8,128)(2,1)S(1)}, bf16[696,256]{1,0:T(8,128)(2,1)S(1)}, u32[]{:S(2)}, u32[]{:S(2)}) collective-permute-start(bf16[696,256]{1,0:T(8,128)(2,1)S(1)} %get-tuple-element.14.own_ref), channel_id=1, source_target_pairs={{4,0},{14,2},{8,4},{2,6},{12,8},{6,10},{0,12},{10,14},{5,1},{15,3}... | collective-permute-start | bytes 1069064 | tf_op jit(solution)/shard_map/ppermute | solution.py:326
  6.4 1.1 %copy-done = bf16[1,2,256,3,216]{2,4,3,1,0:T(8,128)(2,1)S(1)} copy-done((bf16[1,2,256,3,216]{2,4,3,1,0:T(8,128)(2,1)S(1)}, bf16[1,2,256,3,216]{2,4,3,1,0:T(8,128)(2,1)}, u32[]{:S(2)}) %copy-start) | copy-done | bytes 663576
  7.5 0.7 %copy-done.1 = bf16[1,3,3,3,2,216]{5,4,3,2,1,0:T(2,128)(2,1)S(1)} copy-done((bf16[1,3,3,3,2,216]{5,4,3,2,1,0:T(2,128)(2,1)S(1)}, bf16[1,3,3,3,2,216]{5,4,3,2,1,0:T(2,128)(2,1)}, u32[]{:S(2)}) %copy-start.1) | copy-done | bytes 23352
  8.2 3.2 %shard_map.48.flat_ref = bf16[512,256]{1,0:T(8,128)(2,1)S(1)} custom-call(bf16[1296,256]{1,0:T(8,128)(2,1)S(1)} %bitcast.9, bf16[27,2,216]{2,1,0:T(2,128)(2,1)S(1)} %bitcast.11), custom_call_target="tpu_custom_call" | custom-call | flops 700000000 | bytes 8000000 | tf_op jit(solution)/shard_map/pallas_call | solution.py:333
  11.4 2.5 %collective-permute-done.along_ref = bf16[696,256]{1,0:T(8,128)(2,1)S(1)} collective-permute-done((bf16[696,256]{1,0:T(8,128)(2,1)S(1)}, bf16[696,256]{1,0:T(8,128)(2,1)S(1)}, u32[]{:S(2)}, u32[]{:S(2)}) %collective-permute-start) | collective-permute-done | bytes 356384 | tf_op jit(solution)/shard_map/ppermute | solution.py:326
  14.0 0.6 %shard_map.47.early_ref = bf16[672,256]{1,0:T(8,128)(2,1)S(1)} custom-call(bf16[696,256]{1,0:T(8,128)(2,1)S(1)} %get-tuple-element.14.own_ref, bf16[696,256]{1,0:T(8,128)(2,1)S(1)} %collective-permute-done.along_ref), custom_call_target="tpu_custom_call" | custom-call | flops 20000000 | bytes 1000000 | tf_op jit(solution)/shard_map/pallas_call | solution.py:355
  14.5 1.6 %collective-permute-done.1.across_ref = bf16[696,256]{1,0:T(8,128)(2,1)S(1)} collective-permute-done((bf16[696,256]{1,0:T(8,128)(2,1)S(1)}, bf16[696,256]{1,0:T(8,128)(2,1)S(1)}, u32[]{:S(2)}, u32[]{:S(2)}) %collective-permute-start.1) | collective-permute-done | bytes 356384 | tf_op jit(solution)/shard_map/ppermute | solution.py:325
  16.2 1.2 %shard_map.49 = (bf16[192,256]{1,0:T(8,128)(2,1)S(1)}, bf16[192,256]{1,0:T(8,128)(2,1)S(1)}, bf16[192,256]{1,0:T(8,128)(2,1)S(1)}, bf16[192,256]{1,0:T(8,128)(2,1)S(1)}) custom-call(bf16[672,256]{1,0:T(8,128)(2,1)S(1)} %shard_map.47.early_ref, bf16[696,256]{1,0:T(8,128)(2,1)S(1)} %get-tuple-element.14.own_ref, ...), custom_call_target="tpu_custom_call" | custom-call | flops 400000000 | bytes 2000000 | tf_op jit(solution)/shard_map/pallas_call | solution.py:365
  17.4 0.5 %collective-permute-start.2 = (bf16[192,256]{1,0:T(8,128)(2,1)S(1)}, bf16[192,256]{1,0:T(8,128)(2,1)S(1)}, u32[]{:S(2)}, u32[]{:S(2)}) collective-permute-start(bf16[192,256]{1,0:T(8,128)(2,1)S(1)} %get-tuple-element.17), channel_id=1, source_target_pairs={{0,6},{2,4},{4,2},{6,0},{8,14},{10,12},{12,10},{14,8},{1,7},{3,5},... | collective-permute-start | bytes 294920 | tf_op jit(solution)/shard_map/ppermute | solution.py:284
  18.0 1.6 %collective-permute-start.3 = (bf16[192,256]{1,0:T(8,128)(2,1)S(1)}, bf16[192,256]{1,0:T(8,128)(2,1)S(1)}, u32[]{:S(2)}, u32[]{:S(2)}) collective-permute-start(bf16[192,256]{1,0:T(8,128)(2,1)S(1)} %get-tuple-element.18), channel_id=1, source_target_pairs={{0,4},{2,6},{4,0},{6,2},{8,12},{10,14},{12,8},{14,10},{1,5},{3,7},... | collective-permute-start | bytes 294920 | tf_op jit(solution)/shard_map/ppermute | solution.py:284
  19.6 1.4 %collective-permute-start.4 = (bf16[192,256]{1,0:T(8,128)(2,1)S(1)}, bf16[192,256]{1,0:T(8,128)(2,1)S(1)}, u32[]{:S(2)}, u32[]{:S(2)}) collective-permute-start(bf16[192,256]{1,0:T(8,128)(2,1)S(1)} %get-tuple-element.19), channel_id=1, source_target_pairs={{0,2},{2,0},{4,6},{6,4},{8,10},{10,8},{12,14},{14,12},{1,3},{3,1},... | collective-permute-start | bytes 294920 | tf_op jit(solution)/shard_map/ppermute | solution.py:284
  21.0 2.0 %collective-permute-done.2 = bf16[192,256]{1,0:T(8,128)(2,1)S(1)} collective-permute-done((bf16[192,256]{1,0:T(8,128)(2,1)S(1)}, bf16[192,256]{1,0:T(8,128)(2,1)S(1)}, u32[]{:S(2)}, u32[]{:S(2)}) %collective-permute-start.2) | collective-permute-done | bytes 98336 | tf_op jit(solution)/shard_map/ppermute | solution.py:284
  23.0 0.4 collective-permute-done.3
  23.4 0.8 %collective-permute-done.4 = bf16[192,256]{1,0:T(8,128)(2,1)S(1)} collective-permute-done((bf16[192,256]{1,0:T(8,128)(2,1)S(1)}, bf16[192,256]{1,0:T(8,128)(2,1)S(1)}, u32[]{:S(2)}, u32[]{:S(2)}) %collective-permute-start.4) | collective-permute-done | bytes 98336 | tf_op jit(solution)/shard_map/ppermute | solution.py:284
  24.2 1.5 %collective-permute-start.5 = (bf16[192,256]{1,0:T(8,128)(2,1)S(1)}, bf16[192,256]{1,0:T(8,128)(2,1)S(1)}, u32[]{:S(2)}, u32[]{:S(2)}) collective-permute-start(bf16[192,256]{1,0:T(8,128)(2,1)S(1)} %fusion), channel_id=1, source_target_pairs={{0,8},{2,10},{4,12},{6,14},{8,0},{10,2},{12,4},{14,6},{1,9},{3,11}... | collective-permute-start | bytes 294920 | tf_op jit(solution)/shard_map/ppermute | solution.py:284
  25.7 5.0 %collective-permute-done.5 = bf16[192,256]{1,0:T(8,128)(2,1)S(1)} collective-permute-done((bf16[192,256]{1,0:T(8,128)(2,1)S(1)}, bf16[192,256]{1,0:T(8,128)(2,1)S(1)}, u32[]{:S(2)}, u32[]{:S(2)}) %collective-permute-start.5) | collective-permute-done | bytes 98336 | tf_op jit(solution)/shard_map/ppermute | solution.py:284
  30.8 1.4 %collective-permute-start.6 = (bf16[192,256]{1,0:T(8,128)(2,1)S(1)}, bf16[192,256]{1,0:T(8,128)(2,1)S(1)}, u32[]{:S(2)}, u32[]{:S(2)}) collective-permute-start(bf16[192,256]{1,0:T(8,128)(2,1)S(1)} %add_convert_fusion.refs_0_), channel_id=1, source_target_pairs={{0,2},{2,0},{4,6},{6,4},{8,10},{10,8},{12,14},{14,12},{1,3},{3,1},... | collective-permute-start | bytes 294920 | tf_op jit(solution)/shard_map/ppermute | solution.py:284
  32.2 2.2 %collective-permute-start.8 = (bf16[192,256]{1,0:T(8,128)(2,1)S(1)}, bf16[192,256]{1,0:T(8,128)(2,1)S(1)}, u32[]{:S(2)}, u32[]{:S(2)}) collective-permute-start(bf16[192,256]{1,0:T(8,128)(2,1)S(1)} %add_convert_fusion.refs_0_), channel_id=1, source_target_pairs={{0,6},{2,4},{4,2},{6,0},{8,14},{10,12},{12,10},{14,8},{1,7},{3,5},... | collective-permute-start | bytes 294920 | tf_op jit(solution)/shard_map/ppermute | solution.py:284
  34.4 1.0 %shard_map.50 = (bf16[1024,256]{1,0:T(8,128)(2,1)S(1)}, bf16[1024,256]{1,0:T(8,128)(2,1)S(1)}, bf16[256,256]{1,0:T(8,128)(2,1)S(1)}) custom-call(bf16[2,128,1024]{2,1,0:T(8,128)(2,1)S(1)} %collective-permute-done.9.p_ref), custom_call_target="tpu_custom_call" | custom-call | flops 500000000 | bytes 2000000 | tf_op jit(solution)/shard_map/pallas_call | solution.py:343
  35.3 0.1 collective-permute-done.6.refs_1_
  35.5 1.3 %collective-permute-done.7.refs_2_ = bf16[192,256]{1,0:T(8,128)(2,1)S(1)} collective-permute-done((bf16[192,256]{1,0:T(8,128)(2,1)S(1)}, bf16[192,256]{1,0:T(8,128)(2,1)S(1)}, u32[]{:S(2)}, u32[]{:S(2)}) %collective-permute-start.7) | collective-permute-done | bytes 98336 | tf_op jit(solution)/shard_map/ppermute | solution.py:284
  36.8 1.2 %collective-permute-done.8.refs_3_ = bf16[192,256]{1,0:T(8,128)(2,1)S(1)} collective-permute-done((bf16[192,256]{1,0:T(8,128)(2,1)S(1)}, bf16[192,256]{1,0:T(8,128)(2,1)S(1)}, u32[]{:S(2)}, u32[]{:S(2)}) %collective-permute-start.8) | collective-permute-done | bytes 98336 | tf_op jit(solution)/shard_map/ppermute | solution.py:284
  38.0 3.0 %shard_map.51 = bf16[3,2,128,1024]{3,2,1,0:T(8,128)(2,1)} custom-call(s32[3]{0:T(128)S(1)} %copy-done.2, bf16[192,256]{1,0:T(8,128)(2,1)S(1)} %add_convert_fusion.refs_0_, bf16[192,256]{1,0:T(8,128)(2,1)S(1)} %collective-permute-done.6.refs_1_, bf16[192,256]{1,0:T(8,128)(2,1)S(1)} %collective-permute-done.7.refs_2_, ...), custom_call_target="tpu_custom_call" | custom-call | flops 2400000000 | bytes 3000000 | tf_op jit(solution)/shard_map/pallas_call | solution.py:264
  (12 shorter events, 0.1 us)
Async XLA Ops:
  1.2 12.7 %collective-permute-start = (bf16[696,256]{1,0:T(8,128)(2,1)S(1)}, bf16[696,256]{1,0:T(8,128)(2,1)S(1)}, u32[]{:S(2)}, u32[]{:S(2)}) collective-permute-start(bf16[696,256]{1,0:T(8,128)(2,1)S(1)} %get-tuple-element.14.own_ref), channel_id=1, source_target_pairs={{4,0},{14,2},{8,4},{2,6},{12,8},{6,10},{0,12},{10,14},{5,1},{15,3}... | collective-permute-start | bytes 1069064 | tf_op jit(solution)/shard_map/ppermute | solution.py:326
  6.4 9.8 %collective-permute-start.1 = (bf16[696,256]{1,0:T(8,128)(2,1)S(1)}, bf16[696,256]{1,0:T(8,128)(2,1)S(1)}, u32[]{:S(2)}, u32[]{:S(2)}) collective-permute-start(bf16[696,256]{1,0:T(8,128)(2,1)S(1)} %get-tuple-element.15), channel_id=1, source_target_pairs={{0,2},{2,0},{4,6},{6,4},{8,10},{10,8},{12,14},{14,12},{1,3},{3,1},... | collective-permute-start | bytes 1069064 | tf_op jit(solution)/shard_map/ppermute | solution.py:325
  6.4 1.1 %copy-start = (bf16[1,2,256,3,216]{2,4,3,1,0:T(8,128)(2,1)S(1)}, bf16[1,2,256,3,216]{2,4,3,1,0:T(8,128)(2,1)}, u32[]{:S(2)}) copy-start(bf16[1,2,256,3,216]{2,4,3,1,0:T(8,128)(2,1)} %param.4) | copy-start | bytes 1990660
  7.5 0.7 %copy-start.1 = (bf16[1,3,3,3,2,216]{5,4,3,2,1,0:T(2,128)(2,1)S(1)}, bf16[1,3,3,3,2,216]{5,4,3,2,1,0:T(2,128)(2,1)}, u32[]{:S(2)}) copy-start(bf16[1,3,3,3,2,216]{5,4,3,2,1,0:T(2,128)(2,1)} %param.5) | copy-start | bytes 69988
  11.4 9.6 %copy-start.3 = (bf16[1,2,128,1024]{3,2,1,0:T(8,128)(2,1)S(1)}, bf16[1,2,128,1024]{3,2,1,0:T(8,128)(2,1)}, u32[]{:S(2)}) copy-start(bf16[1,2,128,1024]{3,2,1,0:T(8,128)(2,1)} %param.7) | copy-start | bytes 1572868
  17.4 20.6 %copy-start.2 = (s32[3]{0:T(128)S(1)}, s32[3]{0:T(128)}, u32[]{:S(2)}) copy-start(s32[3]{0:T(128)} %dirs_ref.1) | copy-start | bytes 40
  17.4 5.6 %collective-permute-start.2 = (bf16[192,256]{1,0:T(8,128)(2,1)S(1)}, bf16[192,256]{1,0:T(8,128)(2,1)S(1)}, u32[]{:S(2)}, u32[]{:S(2)}) collective-permute-start(bf16[192,256]{1,0:T(8,128)(2,1)S(1)} %get-tuple-element.17), channel_id=1, source_target_pairs={{0,6},{2,4},{4,2},{6,0},{8,14},{10,12},{12,10},{14,8},{1,7},{3,5},... | collective-permute-start | bytes 294920 | tf_op jit(solution)/shard_map/ppermute | solution.py:284
  18.0 5.4 %collective-permute-start.3 = (bf16[192,256]{1,0:T(8,128)(2,1)S(1)}, bf16[192,256]{1,0:T(8,128)(2,1)S(1)}, u32[]{:S(2)}, u32[]{:S(2)}) collective-permute-start(bf16[192,256]{1,0:T(8,128)(2,1)S(1)} %get-tuple-element.18), channel_id=1, source_target_pairs={{0,4},{2,6},{4,0},{6,2},{8,12},{10,14},{12,8},{14,10},{1,5},{3,7},... | collective-permute-start | bytes 294920 | tf_op jit(solution)/shard_map/ppermute | solution.py:284
  19.6 4.6 %collective-permute-start.4 = (bf16[192,256]{1,0:T(8,128)(2,1)S(1)}, bf16[192,256]{1,0:T(8,128)(2,1)S(1)}, u32[]{:S(2)}, u32[]{:S(2)}) collective-permute-start(bf16[192,256]{1,0:T(8,128)(2,1)S(1)} %get-tuple-element.19), channel_id=1, source_target_pairs={{0,2},{2,0},{4,6},{6,4},{8,10},{10,8},{12,14},{14,12},{1,3},{3,1},... | collective-permute-start | bytes 294920 | tf_op jit(solution)/shard_map/ppermute | solution.py:284
  21.0 13.4 %collective-permute-start.9 = (bf16[2,128,1024]{2,1,0:T(8,128)(2,1)S(1)}, bf16[2,128,1024]{2,1,0:T(8,128)(2,1)S(1)}, u32[]{:S(2)}, u32[]{:S(2)}) collective-permute-start(bf16[2,128,1024]{2,1,0:T(8,128)(2,1)S(1)} %bitcast.12), channel_id=1, source_target_pairs={{1,0},{0,1},{3,2},{2,3},{5,4},{4,5},{7,6},{6,7},{9,8},{8,9},{11,10... | collective-permute-start | bytes 1572872 | tf_op jit(solution)/shard_map/ppermute | solution.py:331
  24.2 6.5 %collective-permute-start.5 = (bf16[192,256]{1,0:T(8,128)(2,1)S(1)}, bf16[192,256]{1,0:T(8,128)(2,1)S(1)}, u32[]{:S(2)}, u32[]{:S(2)}) collective-permute-start(bf16[192,256]{1,0:T(8,128)(2,1)S(1)} %fusion), channel_id=1, source_target_pairs={{0,8},{2,10},{4,12},{6,14},{8,0},{10,2},{12,4},{14,6},{1,9},{3,11}... | collective-permute-start | bytes 294920 | tf_op jit(solution)/shard_map/ppermute | solution.py:284
  30.8 4.7 %collective-permute-start.6 = (bf16[192,256]{1,0:T(8,128)(2,1)S(1)}, bf16[192,256]{1,0:T(8,128)(2,1)S(1)}, u32[]{:S(2)}, u32[]{:S(2)}) collective-permute-start(bf16[192,256]{1,0:T(8,128)(2,1)S(1)} %add_convert_fusion.refs_0_), channel_id=1, source_target_pairs={{0,2},{2,0},{4,6},{6,4},{8,10},{10,8},{12,14},{14,12},{1,3},{3,1},... | collective-permute-start | bytes 294920 | tf_op jit(solution)/shard_map/ppermute | solution.py:284
  32.2 4.6 %collective-permute-start.7 = (bf16[192,256]{1,0:T(8,128)(2,1)S(1)}, bf16[192,256]{1,0:T(8,128)(2,1)S(1)}, u32[]{:S(2)}, u32[]{:S(2)}) collective-permute-start(bf16[192,256]{1,0:T(8,128)(2,1)S(1)} %add_convert_fusion.refs_0_), channel_id=1, source_target_pairs={{0,4},{2,6},{4,0},{6,2},{8,12},{10,14},{12,8},{14,10},{1,5},{3,7},... | collective-permute-start | bytes 294920 | tf_op jit(solution)/shard_map/ppermute | solution.py:284
  32.2 5.8 %collective-permute-start.8 = (bf16[192,256]{1,0:T(8,128)(2,1)S(1)}, bf16[192,256]{1,0:T(8,128)(2,1)S(1)}, u32[]{:S(2)}, u32[]{:S(2)}) collective-permute-start(bf16[192,256]{1,0:T(8,128)(2,1)S(1)} %add_convert_fusion.refs_0_), channel_id=1, source_target_pairs={{0,6},{2,4},{4,2},{6,0},{8,14},{10,12},{12,10},{14,8},{1,7},{3,5},... | collective-permute-start | bytes 294920 | tf_op jit(solution)/shard_map/ppermute | solution.py:284
where the time goes:
time: 41.3 us; the launch traced here: 41 us
  waiting for transfers between devices  15 us (36%)
  starting transfers between devices  13.7 us (33%)
  Pallas kernels  10.2 us (25%)
  local copies, waits for them, and re-layouts  1.85 us (4%)
    ppermute x7, waiting for transfers between devices, swap(): lax.ppermute(block, 'space', [(i, i ^ distance) for i in range(ranks)])  10.9 us
    ppermute x7, starting transfers between devices, swap(): lax.ppermute(block, 'space', [(i, i ^ distance) for i in range(ranks)])  8.61 us
    ppermute x1, starting transfers between devices, blocks(): lax.ppermute(along, 'space', [((i + 2) % ranks if i % 2 == 0 else (i - 2)...  5.13 us
    pallas_call x1, Pallas kernels, blocks(): pl.pallas_call(functools.partial(front_kernel, sites), out_shape=jax.Shap...  3.18 us
    pallas_call x1, Pallas kernels, last_call(): pl.pallas_call(functools.partial(last_kernel, near), in_specs=[pl.BlockSp...  2.98 us
    ppermute x1, waiting for transfers between devices, blocks(): lax.ppermute(along, 'space', [((i + 2) % ranks if i % 2 == 0 else (i - 2)...  2.54 us
    unnamed x8, local copies, waits for them, and re-layouts  1.85 us
    ppermute x1, waiting for transfers between devices, blocks(): lax.ppermute(across, 'space', [(i, i ^ 1) for i in range(ranks)])  1.62 us
  transfers between devices with their start and end apart: 10, of which 9 were waited for; matrix products, arithmetic and copies ran while one was open for 0% of the time, Pallas kernels for 12%

commit v1 on v0

--- a/solution.py
+++ b/solution.py
@@ -75,16 +75,16 @@
     fetch = pltpu.make_async_copy(u_ref.at[pl.ds(9, 9)], link_ref, link_sem)
     fetch.start()
     copies = []
-    for slot, (ref, upper) in enumerate(((across_ref, 1 - parity), (along_ref, parity))):
-        for comp in range(6):
-            first = pl.multiple_of(comp * sites + upper * (sites - half), 8)
-            copy = pltpu.make_async_copy(
-                v_ref.at[pl.ds(first, half)],
-                ref.at[pl.ds(comp * half, half)],
-                sems.at[slot, comp],
-            )
-            copy.start()
-            copies.append(copy)
+    source = v_ref.reshape(6, sites, vectors)
+    for slot, (ref, upper) in enumerate(((along_ref, parity), (across_ref, 1 - parity))):
+        first = pl.multiple_of(upper * (sites - half), 8)
+        copy = pltpu.make_async_copy(
+            source.at[:, pl.ds(first, half)],
+            ref.at[pl.ds(0, 6 * half)].reshape(6, half, vectors),
+            sems.at[slot, 0],
+        )
+        copy.start()
+        copies.append(copy)
     fetch.wait()
     links = link_table(link_ref, 0, 9)
     rows = across_ref.shape[0] - 6 * half

time: 41.3 us -> 41.3 us (level)
  no operation moved by 1% of the time
where the time goes in v1:
time: 41.3 us; the launch traced here: 41 us
  waiting for transfers between devices  15.1 us (37%)
  starting transfers between devices  13.7 us (33%)
  Pallas kernels  10.2 us (25%)
  local copies, waits for them, and re-layouts  1.85 us (4%)
    ppermute x7, waiting for transfers between devices, swap(): lax.ppermute(block, 'space', [(i, i ^ distance) for i in range(ranks)])  10.9 us
    ppermute x7, starting transfers between devices, swap(): lax.ppermute(block, 'space', [(i, i ^ distance) for i in range(ranks)])  8.61 us
    ppermute x1, starting transfers between devices, blocks(): lax.ppermute(along, 'space', [((i + 2) % ranks if i % 2 == 0 else (i - 2)...  5.13 us
    pallas_call x1, Pallas kernels, blocks(): pl.pallas_call(functools.partial(front_kernel, sites), out_shape=jax.Shap...  3.18 us
    pallas_call x1, Pallas kernels, last_call(): pl.pallas_call(functools.partial(last_kernel, near), in_specs=[pl.BlockSp...  2.98 us
    ppermute x1, waiting for transfers between devices, blocks(): lax.ppermute(along, 'space', [((i + 2) % ranks if i % 2 == 0 else (i - 2)...  2.54 us
    unnamed x8, local copies, waits for them, and re-layouts  1.85 us
    ppermute x1, waiting for transfers between devices, blocks(): lax.ppermute(across, 'space', [(i, i ^ 1) for i in range(ranks)])  1.63 us
  transfers between devices with their start and end apart: 10, of which 9 were waited for; matrix products, arithmetic and copies ran while one was open for 0% of the time, Pallas kernels for 12%

profile of v1, /device:TPU:0, one launch (start us, length us, event | category | flops | bytes accessed | tf_op | source)
XLA Modules:
  0.0 41.0 jit_solution(14316306112255288347)
XLA Ops:
  0.0 1.2 %shard_map.46 = (bf16[696,256]{1,0:T(8,128)(2,1)S(1)}, bf16[696,256]{1,0:T(8,128)(2,1)S(1)}) custom-call(bf16[1296,256]{1,0:T(8,128)(2,1)} %bitcast.8, bf16[27,2,216]{2,1,0:T(2,128)(2,1)} %bitcast.10), custom_call_target="tpu_custom_call" | custom-call | tf_op jit(solution)/shard_map/pallas_call | solution.py:313
  1.2 5.1 %collective-permute-start = (bf16[696,256]{1,0:T(8,128)(2,1)S(1)}, bf16[696,256]{1,0:T(8,128)(2,1)S(1)}, u32[]{:S(2)}, u32[]{:S(2)}) collective-permute-start(bf16[696,256]{1,0:T(8,128)(2,1)S(1)} %get-tuple-element.14.own_ref), channel_id=1, source_target_pairs={{4,0},{14,2},{8,4},{2,6},{12,8},{6,10},{0,12},{10,14},{5,1},{15,3}... | collective-permute-start | bytes 1069064 | tf_op jit(solution)/shard_map/ppermute | solution.py:326
  6.4 1.1 %copy-done = bf16[1,2,256,3,216]{2,4,3,1,0:T(8,128)(2,1)S(1)} copy-done((bf16[1,2,256,3,216]{2,4,3,1,0:T(8,128)(2,1)S(1)}, bf16[1,2,256,3,216]{2,4,3,1,0:T(8,128)(2,1)}, u32[]{:S(2)}) %copy-start) | copy-done | bytes 663576
  7.4 0.7 %copy-done.1 = bf16[1,3,3,3,2,216]{5,4,3,2,1,0:T(2,128)(2,1)S(1)} copy-done((bf16[1,3,3,3,2,216]{5,4,3,2,1,0:T(2,128)(2,1)S(1)}, bf16[1,3,3,3,2,216]{5,4,3,2,1,0:T(2,128)(2,1)}, u32[]{:S(2)}) %copy-start.1) | copy-done | bytes 23352
  8.2 3.2 %shard_map.48.flat_ref = bf16[512,256]{1,0:T(8,128)(2,1)S(1)} custom-call(bf16[1296,256]{1,0:T(8,128)(2,1)S(1)} %bitcast.9, bf16[27,2,216]{2,1,0:T(2,128)(2,1)S(1)} %bitcast.11), custom_call_target="tpu_custom_call" | custom-call | flops 700000000 | bytes 8000000 | tf_op jit(solution)/shard_map/pallas_call | solution.py:333
  11.4 2.5 %collective-permute-done.along_ref = bf16[696,256]{1,0:T(8,128)(2,1)S(1)} collective-permute-done((bf16[696,256]{1,0:T(8,128)(2,1)S(1)}, bf16[696,256]{1,0:T(8,128)(2,1)S(1)}, u32[]{:S(2)}, u32[]{:S(2)}) %collective-permute-start) | collective-permute-done | bytes 356384 | tf_op jit(solution)/shard_map/ppermute | solution.py:326
  13.9 0.6 %shard_map.47.early_ref = bf16[672,256]{1,0:T(8,128)(2,1)S(1)} custom-call(bf16[696,256]{1,0:T(8,128)(2,1)S(1)} %get-tuple-element.14.own_ref, bf16[696,256]{1,0:T(8,128)(2,1)S(1)} %collective-permute-done.along_ref), custom_call_target="tpu_custom_call" | custom-call | flops 20000000 | bytes 1000000 | tf_op jit(solution)/shard_map/pallas_call | solution.py:355
  14.5 1.6 %collective-permute-done.1.across_ref = bf16[696,256]{1,0:T(8,128)(2,1)S(1)} collective-permute-done((bf16[696,256]{1,0:T(8,128)(2,1)S(1)}, bf16[696,256]{1,0:T(8,128)(2,1)S(1)}, u32[]{:S(2)}, u32[]{:S(2)}) %collective-permute-start.1) | collective-permute-done | bytes 356384 | tf_op jit(solution)/shard_map/ppermute | solution.py:325
  16.1 1.2 %shard_map.49 = (bf16[192,256]{1,0:T(8,128)(2,1)S(1)}, bf16[192,256]{1,0:T(8,128)(2,1)S(1)}, bf16[192,256]{1,0:T(8,128)(2,1)S(1)}, bf16[192,256]{1,0:T(8,128)(2,1)S(1)}) custom-call(bf16[672,256]{1,0:T(8,128)(2,1)S(1)} %shard_map.47.early_ref, bf16[696,256]{1,0:T(8,128)(2,1)S(1)} %get-tuple-element.14.own_ref, ...), custom_call_target="tpu_custom_call" | custom-call | flops 400000000 | bytes 2000000 | tf_op jit(solution)/shard_map/pallas_call | solution.py:365
  17.4 0.6 %collective-permute-start.2 = (bf16[192,256]{1,0:T(8,128)(2,1)S(1)}, bf16[192,256]{1,0:T(8,128)(2,1)S(1)}, u32[]{:S(2)}, u32[]{:S(2)}) collective-permute-start(bf16[192,256]{1,0:T(8,128)(2,1)S(1)} %get-tuple-element.17), channel_id=1, source_target_pairs={{0,6},{2,4},{4,2},{6,0},{8,14},{10,12},{12,10},{14,8},{1,7},{3,5},... | collective-permute-start | bytes 294920 | tf_op jit(solution)/shard_map/ppermute | solution.py:284
  18.0 1.6 %collective-permute-start.3 = (bf16[192,256]{1,0:T(8,128)(2,1)S(1)}, bf16[192,256]{1,0:T(8,128)(2,1)S(1)}, u32[]{:S(2)}, u32[]{:S(2)}) collective-permute-start(bf16[192,256]{1,0:T(8,128)(2,1)S(1)} %get-tuple-element.18), channel_id=1, source_target_pairs={{0,4},{2,6},{4,0},{6,2},{8,12},{10,14},{12,8},{14,10},{1,5},{3,7},... | collective-permute-start | bytes 294920 | tf_op jit(solution)/shard_map/ppermute | solution.py:284
  19.5 1.4 %collective-permute-start.4 = (bf16[192,256]{1,0:T(8,128)(2,1)S(1)}, bf16[192,256]{1,0:T(8,128)(2,1)S(1)}, u32[]{:S(2)}, u32[]{:S(2)}) collective-permute-start(bf16[192,256]{1,0:T(8,128)(2,1)S(1)} %get-tuple-element.19), channel_id=1, source_target_pairs={{0,2},{2,0},{4,6},{6,4},{8,10},{10,8},{12,14},{14,12},{1,3},{3,1},... | collective-permute-start | bytes 294920 | tf_op jit(solution)/shard_map/ppermute | solution.py:284
  21.0 2.0 %collective-permute-done.2 = bf16[192,256]{1,0:T(8,128)(2,1)S(1)} collective-permute-done((bf16[192,256]{1,0:T(8,128)(2,1)S(1)}, bf16[192,256]{1,0:T(8,128)(2,1)S(1)}, u32[]{:S(2)}, u32[]{:S(2)}) %collective-permute-start.2) | collective-permute-done | bytes 98336 | tf_op jit(solution)/shard_map/ppermute | solution.py:284
  23.0 0.4 collective-permute-done.3
  23.4 0.8 %collective-permute-done.4 = bf16[192,256]{1,0:T(8,128)(2,1)S(1)} collective-permute-done((bf16[192,256]{1,0:T(8,128)(2,1)S(1)}, bf16[192,256]{1,0:T(8,128)(2,1)S(1)}, u32[]{:S(2)}, u32[]{:S(2)}) %collective-permute-start.4) | collective-permute-done | bytes 98336 | tf_op jit(solution)/shard_map/ppermute | solution.py:284
  24.2 1.5 %collective-permute-start.5 = (bf16[192,256]{1,0:T(8,128)(2,1)S(1)}, bf16[192,256]{1,0:T(8,128)(2,1)S(1)}, u32[]{:S(2)}, u32[]{:S(2)}) collective-permute-start(bf16[192,256]{1,0:T(8,128)(2,1)S(1)} %fusion), channel_id=1, source_target_pairs={{0,8},{2,10},{4,12},{6,14},{8,0},{10,2},{12,4},{14,6},{1,9},{3,11}... | collective-permute-start | bytes 294920 | tf_op jit(solution)/shard_map/ppermute | solution.py:284
  25.7 5.1 %collective-permute-done.5 = bf16[192,256]{1,0:T(8,128)(2,1)S(1)} collective-permute-done((bf16[192,256]{1,0:T(8,128)(2,1)S(1)}, bf16[192,256]{1,0:T(8,128)(2,1)S(1)}, u32[]{:S(2)}, u32[]{:S(2)}) %collective-permute-start.5) | collective-permute-done | bytes 98336 | tf_op jit(solution)/shard_map/ppermute | solution.py:284
  30.9 1.3 %collective-permute-start.6 = (bf16[192,256]{1,0:T(8,128)(2,1)S(1)}, bf16[192,256]{1,0:T(8,128)(2,1)S(1)}, u32[]{:S(2)}, u32[]{:S(2)}) collective-permute-start(bf16[192,256]{1,0:T(8,128)(2,1)S(1)} %add_convert_fusion.refs_0_), channel_id=1, source_target_pairs={{0,2},{2,0},{4,6},{6,4},{8,10},{10,8},{12,14},{14,12},{1,3},{3,1},... | collective-permute-start | bytes 294920 | tf_op jit(solution)/shard_map/ppermute | solution.py:284
  32.2 2.2 %collective-permute-start.8 = (bf16[192,256]{1,0:T(8,128)(2,1)S(1)}, bf16[192,256]{1,0:T(8,128)(2,1)S(1)}, u32[]{:S(2)}, u32[]{:S(2)}) collective-permute-start(bf16[192,256]{1,0:T(8,128)(2,1)S(1)} %add_convert_fusion.refs_0_), channel_id=1, source_target_pairs={{0,6},{2,4},{4,2},{6,0},{8,14},{10,12},{12,10},{14,8},{1,7},{3,5},... | collective-permute-start | bytes 294920 | tf_op jit(solution)/shard_map/ppermute | solution.py:284
  34.4 1.0 %shard_map.50 = (bf16[1024,256]{1,0:T(8,128)(2,1)S(1)}, bf16[1024,256]{1,0:T(8,128)(2,1)S(1)}, bf16[256,256]{1,0:T(8,128)(2,1)S(1)}) custom-call(bf16[2,128,1024]{2,1,0:T(8,128)(2,1)S(1)} %collective-permute-done.9.p_ref), custom_call_target="tpu_custom_call" | custom-call | flops 500000000 | bytes 2000000 | tf_op jit(solution)/shard_map/pallas_call | solution.py:343
  35.4 0.1 collective-permute-done.6.refs_1_
  35.5 1.2 %collective-permute-done.7.refs_2_ = bf16[192,256]{1,0:T(8,128)(2,1)S(1)} collective-permute-done((bf16[192,256]{1,0:T(8,128)(2,1)S(1)}, bf16[192,256]{1,0:T(8,128)(2,1)S(1)}, u32[]{:S(2)}, u32[]{:S(2)}) %collective-permute-start.7) | collective-permute-done | bytes 98336 | tf_op jit(solution)/shard_map/ppermute | solution.py:284
  36.8 1.3 %collective-permute-done.8.refs_3_ = bf16[192,256]{1,0:T(8,128)(2,1)S(1)} collective-permute-done((bf16[192,256]{1,0:T(8,128)(2,1)S(1)}, bf16[192,256]{1,0:T(8,128)(2,1)S(1)}, u32[]{:S(2)}, u32[]{:S(2)}) %collective-permute-start.8) | collective-permute-done | bytes 98336 | tf_op jit(solution)/shard_map/ppermute | solution.py:284
  38.1 3.0 %shard_map.51 = bf16[3,2,128,1024]{3,2,1,0:T(8,128)(2,1)} custom-call(s32[3]{0:T(128)S(1)} %copy-done.2, bf16[192,256]{1,0:T(8,128)(2,1)S(1)} %add_convert_fusion.refs_0_, bf16[192,256]{1,0:T(8,128)(2,1)S(1)} %collective-permute-done.6.refs_1_, bf16[192,256]{1,0:T(8,128)(2,1)S(1)} %collective-permute-done.7.refs_2_, ...), custom_call_target="tpu_custom_call" | custom-call | flops 2400000000 | bytes 3000000 | tf_op jit(solution)/shard_map/pallas_call | solution.py:264
  (12 shorter events, 0.1 us)
Async XLA Ops:
  1.2 12.7 %collective-permute-start = (bf16[696,256]{1,0:T(8,128)(2,1)S(1)}, bf16[696,256]{1,0:T(8,128)(2,1)S(1)}, u32[]{:S(2)}, u32[]{:S(2)}) collective-permute-start(bf16[696,256]{1,0:T(8,128)(2,1)S(1)} %get-tuple-element.14.own_ref), channel_id=1, source_target_pairs={{4,0},{14,2},{8,4},{2,6},{12,8},{6,10},{0,12},{10,14},{5,1},{15,3}... | collective-permute-start | bytes 1069064 | tf_op jit(solution)/shard_map/ppermute | solution.py:326
  6.4 9.8 %collective-permute-start.1 = (bf16[696,256]{1,0:T(8,128)(2,1)S(1)}, bf16[696,256]{1,0:T(8,128)(2,1)S(1)}, u32[]{:S(2)}, u32[]{:S(2)}) collective-permute-start(bf16[696,256]{1,0:T(8,128)(2,1)S(1)} %get-tuple-element.15), channel_id=1, source_target_pairs={{0,2},{2,0},{4,6},{6,4},{8,10},{10,8},{12,14},{14,12},{1,3},{3,1},... | collective-permute-start | bytes 1069064 | tf_op jit(solution)/shard_map/ppermute | solution.py:325
  6.4 1.1 %copy-start = (bf16[1,2,256,3,216]{2,4,3,1,0:T(8,128)(2,1)S(1)}, bf16[1,2,256,3,216]{2,4,3,1,0:T(8,128)(2,1)}, u32[]{:S(2)}) copy-start(bf16[1,2,256,3,216]{2,4,3,1,0:T(8,128)(2,1)} %param.4) | copy-start | bytes 1990660
  7.4 0.7 %copy-start.1 = (bf16[1,3,3,3,2,216]{5,4,3,2,1,0:T(2,128)(2,1)S(1)}, bf16[1,3,3,3,2,216]{5,4,3,2,1,0:T(2,128)(2,1)}, u32[]{:S(2)}) copy-start(bf16[1,3,3,3,2,216]{5,4,3,2,1,0:T(2,128)(2,1)} %param.5) | copy-start | bytes 69988
  11.4 9.6 %copy-start.3 = (bf16[1,2,128,1024]{3,2,1,0:T(8,128)(2,1)S(1)}, bf16[1,2,128,1024]{3,2,1,0:T(8,128)(2,1)}, u32[]{:S(2)}) copy-start(bf16[1,2,128,1024]{3,2,1,0:T(8,128)(2,1)} %param.7) | copy-start | bytes 1572868
  17.4 20.7 %copy-start.2 = (s32[3]{0:T(128)S(1)}, s32[3]{0:T(128)}, u32[]{:S(2)}) copy-start(s32[3]{0:T(128)} %dirs_ref.1) | copy-start | bytes 40
  17.4 5.6 %collective-permute-start.2 = (bf16[192,256]{1,0:T(8,128)(2,1)S(1)}, bf16[192,256]{1,0:T(8,128)(2,1)S(1)}, u32[]{:S(2)}, u32[]{:S(2)}) collective-permute-start(bf16[192,256]{1,0:T(8,128)(2,1)S(1)} %get-tuple-element.17), channel_id=1, source_target_pairs={{0,6},{2,4},{4,2},{6,0},{8,14},{10,12},{12,10},{14,8},{1,7},{3,5},... | collective-permute-start | bytes 294920 | tf_op jit(solution)/shard_map/ppermute | solution.py:284
  18.0 5.4 %collective-permute-start.3 = (bf16[192,256]{1,0:T(8,128)(2,1)S(1)}, bf16[192,256]{1,0:T(8,128)(2,1)S(1)}, u32[]{:S(2)}, u32[]{:S(2)}) collective-permute-start(bf16[192,256]{1,0:T(8,128)(2,1)S(1)} %get-tuple-element.18), channel_id=1, source_target_pairs={{0,4},{2,6},{4,0},{6,2},{8,12},{10,14},{12,8},{14,10},{1,5},{3,7},... | collective-permute-start | bytes 294920 | tf_op jit(solution)/shard_map/ppermute | solution.py:284
  19.5 4.6 %collective-permute-start.4 = (bf16[192,256]{1,0:T(8,128)(2,1)S(1)}, bf16[192,256]{1,0:T(8,128)(2,1)S(1)}, u32[]{:S(2)}, u32[]{:S(2)}) collective-permute-start(bf16[192,256]{1,0:T(8,128)(2,1)S(1)} %get-tuple-element.19), channel_id=1, source_target_pairs={{0,2},{2,0},{4,6},{6,4},{8,10},{10,8},{12,14},{14,12},{1,3},{3,1},... | collective-permute-start | bytes 294920 | tf_op jit(solution)/shard_map/ppermute | solution.py:284
  21.0 13.5 %collective-permute-start.9 = (bf16[2,128,1024]{2,1,0:T(8,128)(2,1)S(1)}, bf16[2,128,1024]{2,1,0:T(8,128)(2,1)S(1)}, u32[]{:S(2)}, u32[]{:S(2)}) collective-permute-start(bf16[2,128,1024]{2,1,0:T(8,128)(2,1)S(1)} %bitcast.12), channel_id=1, source_target_pairs={{1,0},{0,1},{3,2},{2,3},{5,4},{4,5},{7,6},{6,7},{9,8},{8,9},{11,10... | collective-permute-start | bytes 1572872 | tf_op jit(solution)/shard_map/ppermute | solution.py:331
  24.2 6.6 %collective-permute-start.5 = (bf16[192,256]{1,0:T(8,128)(2,1)S(1)}, bf16[192,256]{1,0:T(8,128)(2,1)S(1)}, u32[]{:S(2)}, u32[]{:S(2)}) collective-permute-start(bf16[192,256]{1,0:T(8,128)(2,1)S(1)} %fusion), channel_id=1, source_target_pairs={{0,8},{2,10},{4,12},{6,14},{8,0},{10,2},{12,4},{14,6},{1,9},{3,11}... | collective-permute-start | bytes 294920 | tf_op jit(solution)/shard_map/ppermute | solution.py:284
  30.9 4.7 %collective-permute-start.6 = (bf16[192,256]{1,0:T(8,128)(2,1)S(1)}, bf16[192,256]{1,0:T(8,128)(2,1)S(1)}, u32[]{:S(2)}, u32[]{:S(2)}) collective-permute-start(bf16[192,256]{1,0:T(8,128)(2,1)S(1)} %add_convert_fusion.refs_0_), channel_id=1, source_target_pairs={{0,2},{2,0},{4,6},{6,4},{8,10},{10,8},{12,14},{14,12},{1,3},{3,1},... | collective-permute-start | bytes 294920 | tf_op jit(solution)/shard_map/ppermute | solution.py:284
  32.2 4.6 %collective-permute-start.7 = (bf16[192,256]{1,0:T(8,128)(2,1)S(1)}, bf16[192,256]{1,0:T(8,128)(2,1)S(1)}, u32[]{:S(2)}, u32[]{:S(2)}) collective-permute-start(bf16[192,256]{1,0:T(8,128)(2,1)S(1)} %add_convert_fusion.refs_0_), channel_id=1, source_target_pairs={{0,4},{2,6},{4,0},{6,2},{8,12},{10,14},{12,8},{14,10},{1,5},{3,7},... | collective-permute-start | bytes 294920 | tf_op jit(solution)/shard_map/ppermute | solution.py:284
  32.2 5.9 %collective-permute-start.8 = (bf16[192,256]{1,0:T(8,128)(2,1)S(1)}, bf16[192,256]{1,0:T(8,128)(2,1)S(1)}, u32[]{:S(2)}, u32[]{:S(2)}) collective-permute-start(bf16[192,256]{1,0:T(8,128)(2,1)S(1)} %add_convert_fusion.refs_0_), channel_id=1, source_target_pairs={{0,6},{2,4},{4,2},{6,0},{8,14},{10,12},{12,10},{14,8},{1,7},{3,5},... | collective-permute-start | bytes 294920 | tf_op jit(solution)/shard_map/ppermute | solution.py:284

commit v2 on v0

--- a/solution.py
+++ b/solution.py
@@ -145,14 +145,15 @@
     even = lax.rem(lax.axis_index("space"), 2) == 0
     rotated(half, across_ref[...], w_ref)
     real, imag = pl.ds(0, 3 * half), pl.ds(3 * half, 3 * half)
-    packed = packed_elemental(
-        early_ref[real, :], early_ref[imag, :], across_ref[real, :], across_ref[imag, :]
-    ) + packed_elemental(
-        w_ref[real, :].astype(BF16),
-        w_ref[imag, :].astype(BF16),
-        jnp.where(even, along_ref[real, :], own_ref[real, :]),
-        jnp.where(even, along_ref[imag, :], own_ref[imag, :]),
-    )
+    left = jnp.concatenate(
+        [early_ref[real, :], early_ref[imag, :], w_ref[real, :], w_ref[imag, :]], axis=0
+    )
+    own_real = jnp.where(even, along_ref[real, :], own_ref[real, :])
+    own_imag = jnp.where(even, along_ref[imag, :], own_ref[imag, :])
+    v_real, v_imag = across_ref[real, :], across_ref[imag, :]
+    re = dot(left, jnp.concatenate([v_real, v_imag, own_real, own_imag], axis=0), 0, 0)
+    im = dot(left, jnp.concatenate([v_imag, -v_real, own_imag, -own_real], axis=0), 0, 0)
+    packed = (re + im) + jnp.transpose(im - re)
     y_ref[...] = packed.astype(BF16)
     place = lax.rem(lax.axis_index("space"), near)
     wide, narrow = flat_ref.shape[0] // near, y_ref.shape[0] // near
@@ -367,7 +368,10 @@
         out_shape=[jax.ShapeDtypeStruct((3 * vectors // near, vectors), BF16)] * near,
         in_specs=[VMEM] * 5,
         out_specs=[VMEM] * near,
-        scratch_shapes=[pltpu.VMEM((6 * half, vectors), F32), pltpu.VMEM((vectors, vectors), BF16)],
+        scratch_shapes=[
+            pltpu.VMEM((6 * half, vectors), BF16),
+            pltpu.VMEM((vectors, vectors), BF16),
+        ],
         cost_estimate=pl.CostEstimate(
             flops=400_000_000, bytes_accessed=2_000_000, transcendentals=0
         ),

time: 41.3 us -> 41.3 us (level)
  no operation moved by 1% of the time
where the time goes in v2:
time: 41.3 us; the launch traced here: 41 us
  waiting for transfers between devices  15.1 us (37%)
  starting transfers between devices  13.7 us (33%)
  Pallas kernels  10.1 us (24%)
  local copies, waits for them, and re-layouts  1.85 us (4%)
    ppermute x7, waiting for transfers between devices, swap(): lax.ppermute(block, 'space', [(i, i ^ distance) for i in range(ranks)])  10.9 us
    ppermute x7, starting transfers between devices, swap(): lax.ppermute(block, 'space', [(i, i ^ distance) for i in range(ranks)])  8.61 us
    ppermute x1, starting transfers between devices, blocks(): lax.ppermute(along, 'space', [((i + 2) % ranks if i % 2 == 0 else (i - 2)...  5.13 us
    pallas_call x1, Pallas kernels, blocks(): pl.pallas_call(functools.partial(front_kernel, sites), out_shape=jax.Shap...  3.18 us
    pallas_call x1, Pallas kernels, last_call(): pl.pallas_call(functools.partial(last_kernel, near), in_specs=[pl.BlockSp...  2.98 us
    ppermute x1, waiting for transfers between devices, blocks(): lax.ppermute(along, 'space', [((i + 2) % ranks if i % 2 == 0 else (i - 2)...  2.54 us
    unnamed x8, local copies, waits for them, and re-layouts  1.85 us
    ppermute x1, waiting for transfers between devices, blocks(): lax.ppermute(across, 'space', [(i, i ^ 1) for i in range(ranks)])  1.62 us
  transfers between devices with their start and end apart: 10, of which 9 were waited for; matrix products, arithmetic and copies ran while one was open for 0% of the time, Pallas kernels for 12%

profile of v2, /device:TPU:0, one launch (start us, length us, event | category | flops | bytes accessed | tf_op | source)
XLA Modules:
  0.0 41.0 jit_solution(3620271457972193795)
XLA Ops:
  0.0 1.2 %shard_map.46 = (bf16[696,256]{1,0:T(8,128)(2,1)S(1)}, bf16[696,256]{1,0:T(8,128)(2,1)S(1)}) custom-call(bf16[1296,256]{1,0:T(8,128)(2,1)} %bitcast.8, bf16[27,2,216]{2,1,0:T(2,128)(2,1)} %bitcast.10), custom_call_target="tpu_custom_call" | custom-call | tf_op jit(solution)/shard_map/pallas_call | solution.py:314
  1.2 5.1 %collective-permute-start = (bf16[696,256]{1,0:T(8,128)(2,1)S(1)}, bf16[696,256]{1,0:T(8,128)(2,1)S(1)}, u32[]{:S(2)}, u32[]{:S(2)}) collective-permute-start(bf16[696,256]{1,0:T(8,128)(2,1)S(1)} %get-tuple-element.14.own_ref), channel_id=1, source_target_pairs={{4,0},{14,2},{8,4},{2,6},{12,8},{6,10},{0,12},{10,14},{5,1},{15,3}... | collective-permute-start | bytes 1069064 | tf_op jit(solution)/shard_map/ppermute | solution.py:327
  6.4 1.1 %copy-done = bf16[1,2,256,3,216]{2,4,3,1,0:T(8,128)(2,1)S(1)} copy-done((bf16[1,2,256,3,216]{2,4,3,1,0:T(8,128)(2,1)S(1)}, bf16[1,2,256,3,216]{2,4,3,1,0:T(8,128)(2,1)}, u32[]{:S(2)}) %copy-start) | copy-done | bytes 663576
  7.5 0.7 %copy-done.1 = bf16[1,3,3,3,2,216]{5,4,3,2,1,0:T(2,128)(2,1)S(1)} copy-done((bf16[1,3,3,3,2,216]{5,4,3,2,1,0:T(2,128)(2,1)S(1)}, bf16[1,3,3,3,2,216]{5,4,3,2,1,0:T(2,128)(2,1)}, u32[]{:S(2)}) %copy-start.1) | copy-done | bytes 23352
  8.2 3.2 %shard_map.48.flat_ref = bf16[512,256]{1,0:T(8,128)(2,1)S(1)} custom-call(bf16[1296,256]{1,0:T(8,128)(2,1)S(1)} %bitcast.9, bf16[27,2,216]{2,1,0:T(2,128)(2,1)S(1)} %bitcast.11), custom_call_target="tpu_custom_call" | custom-call | flops 700000000 | bytes 8000000 | tf_op jit(solution)/shard_map/pallas_call | solution.py:334
  11.4 2.5 %collective-permute-done.along_ref = bf16[696,256]{1,0:T(8,128)(2,1)S(1)} collective-permute-done((bf16[696,256]{1,0:T(8,128)(2,1)S(1)}, bf16[696,256]{1,0:T(8,128)(2,1)S(1)}, u32[]{:S(2)}, u32[]{:S(2)}) %collective-permute-start) | collective-permute-done | bytes 356384 | tf_op jit(solution)/shard_map/ppermute | solution.py:327
  14.0 0.6 %shard_map.47.early_ref = bf16[672,256]{1,0:T(8,128)(2,1)S(1)} custom-call(bf16[696,256]{1,0:T(8,128)(2,1)S(1)} %get-tuple-element.14.own_ref, bf16[696,256]{1,0:T(8,128)(2,1)S(1)} %collective-permute-done.along_ref), custom_call_target="tpu_custom_call" | custom-call | flops 20000000 | bytes 1000000 | tf_op jit(solution)/shard_map/pallas_call | solution.py:356
  14.5 1.6 %collective-permute-done.1.across_ref = bf16[696,256]{1,0:T(8,128)(2,1)S(1)} collective-permute-done((bf16[696,256]{1,0:T(8,128)(2,1)S(1)}, bf16[696,256]{1,0:T(8,128)(2,1)S(1)}, u32[]{:S(2)}, u32[]{:S(2)}) %collective-permute-start.1) | collective-permute-done | bytes 356384 | tf_op jit(solution)/shard_map/ppermute | solution.py:326
  16.2 1.2 %shard_map.49 = (bf16[192,256]{1,0:T(8,128)(2,1)S(1)}, bf16[192,256]{1,0:T(8,128)(2,1)S(1)}, bf16[192,256]{1,0:T(8,128)(2,1)S(1)}, bf16[192,256]{1,0:T(8,128)(2,1)S(1)}) custom-call(bf16[672,256]{1,0:T(8,128)(2,1)S(1)} %shard_map.47.early_ref, bf16[696,256]{1,0:T(8,128)(2,1)S(1)} %get-tuple-element.14.own_ref, ...), custom_call_target="tpu_custom_call" | custom-call | flops 400000000 | bytes 2000000 | tf_op jit(solution)/shard_map/pallas_call | solution.py:366
  17.4 0.5 %collective-permute-start.2 = (bf16[192,256]{1,0:T(8,128)(2,1)S(1)}, bf16[192,256]{1,0:T(8,128)(2,1)S(1)}, u32[]{:S(2)}, u32[]{:S(2)}) collective-permute-start(bf16[192,256]{1,0:T(8,128)(2,1)S(1)} %get-tuple-element.17), channel_id=1, source_target_pairs={{0,6},{2,4},{4,2},{6,0},{8,14},{10,12},{12,10},{14,8},{1,7},{3,5},... | collective-permute-start | bytes 294920 | tf_op jit(solution)/shard_map/ppermute | solution.py:285
  17.9 1.6 %collective-permute-start.3 = (bf16[192,256]{1,0:T(8,128)(2,1)S(1)}, bf16[192,256]{1,0:T(8,128)(2,1)S(1)}, u32[]{:S(2)}, u32[]{:S(2)}) collective-permute-start(bf16[192,256]{1,0:T(8,128)(2,1)S(1)} %get-tuple-element.18), channel_id=1, source_target_pairs={{0,4},{2,6},{4,0},{6,2},{8,12},{10,14},{12,8},{14,10},{1,5},{3,7},... | collective-permute-start | bytes 294920 | tf_op jit(solution)/shard_map/ppermute | solution.py:285
  19.5 1.4 %collective-permute-start.4 = (bf16[192,256]{1,0:T(8,128)(2,1)S(1)}, bf16[192,256]{1,0:T(8,128)(2,1)S(1)}, u32[]{:S(2)}, u32[]{:S(2)}) collective-permute-start(bf16[192,256]{1,0:T(8,128)(2,1)S(1)} %get-tuple-element.19), channel_id=1, source_target_pairs={{0,2},{2,0},{4,6},{6,4},{8,10},{10,8},{12,14},{14,12},{1,3},{3,1},... | collective-permute-start | bytes 294920 | tf_op jit(solution)/shard_map/ppermute | solution.py:285
  21.0 2.0 %collective-permute-done.2 = bf16[192,256]{1,0:T(8,128)(2,1)S(1)} collective-permute-done((bf16[192,256]{1,0:T(8,128)(2,1)S(1)}, bf16[192,256]{1,0:T(8,128)(2,1)S(1)}, u32[]{:S(2)}, u32[]{:S(2)}) %collective-permute-start.2) | collective-permute-done | bytes 98336 | tf_op jit(solution)/shard_map/ppermute | solution.py:285
  23.0 0.4 collective-permute-done.3
  23.4 0.8 %collective-permute-done.4 = bf16[192,256]{1,0:T(8,128)(2,1)S(1)} collective-permute-done((bf16[192,256]{1,0:T(8,128)(2,1)S(1)}, bf16[192,256]{1,0:T(8,128)(2,1)S(1)}, u32[]{:S(2)}, u32[]{:S(2)}) %collective-permute-start.4) | collective-permute-done | bytes 98336 | tf_op jit(solution)/shard_map/ppermute | solution.py:285
  24.2 1.5 %collective-permute-start.5 = (bf16[192,256]{1,0:T(8,128)(2,1)S(1)}, bf16[192,256]{1,0:T(8,128)(2,1)S(1)}, u32[]{:S(2)}, u32[]{:S(2)}) collective-permute-start(bf16[192,256]{1,0:T(8,128)(2,1)S(1)} %fusion), channel_id=1, source_target_pairs={{0,8},{2,10},{4,12},{6,14},{8,0},{10,2},{12,4},{14,6},{1,9},{3,11}... | collective-permute-start | bytes 294920 | tf_op jit(solution)/shard_map/ppermute | solution.py:285
  25.7 5.1 %collective-permute-done.5 = bf16[192,256]{1,0:T(8,128)(2,1)S(1)} collective-permute-done((bf16[192,256]{1,0:T(8,128)(2,1)S(1)}, bf16[192,256]{1,0:T(8,128)(2,1)S(1)}, u32[]{:S(2)}, u32[]{:S(2)}) %collective-permute-start.5) | collective-permute-done | bytes 98336 | tf_op jit(solution)/shard_map/ppermute | solution.py:285
  30.9 1.3 %collective-permute-start.6 = (bf16[192,256]{1,0:T(8,128)(2,1)S(1)}, bf16[192,256]{1,0:T(8,128)(2,1)S(1)}, u32[]{:S(2)}, u32[]{:S(2)}) collective-permute-start(bf16[192,256]{1,0:T(8,128)(2,1)S(1)} %add_convert_fusion.refs_0_), channel_id=1, source_target_pairs={{0,2},{2,0},{4,6},{6,4},{8,10},{10,8},{12,14},{14,12},{1,3},{3,1},... | collective-permute-start | bytes 294920 | tf_op jit(solution)/shard_map/ppermute | solution.py:285
  32.2 2.2 %collective-permute-start.8 = (bf16[192,256]{1,0:T(8,128)(2,1)S(1)}, bf16[192,256]{1,0:T(8,128)(2,1)S(1)}, u32[]{:S(2)}, u32[]{:S(2)}) collective-permute-start(bf16[192,256]{1,0:T(8,128)(2,1)S(1)} %add_convert_fusion.refs_0_), channel_id=1, source_target_pairs={{0,6},{2,4},{4,2},{6,0},{8,14},{10,12},{12,10},{14,8},{1,7},{3,5},... | collective-permute-start | bytes 294920 | tf_op jit(solution)/shard_map/ppermute | solution.py:285
  34.4 1.0 %shard_map.50 = (bf16[1024,256]{1,0:T(8,128)(2,1)S(1)}, bf16[1024,256]{1,0:T(8,128)(2,1)S(1)}, bf16[256,256]{1,0:T(8,128)(2,1)S(1)}) custom-call(bf16[2,128,1024]{2,1,0:T(8,128)(2,1)S(1)} %collective-permute-done.9.p_ref), custom_call_target="tpu_custom_call" | custom-call | flops 500000000 | bytes 2000000 | tf_op jit(solution)/shard_map/pallas_call | solution.py:344
  35.4 0.2 collective-permute-done.6.refs_1_
  35.5 1.3 %collective-permute-done.7.refs_2_ = bf16[192,256]{1,0:T(8,128)(2,1)S(1)} collective-permute-done((bf16[192,256]{1,0:T(8,128)(2,1)S(1)}, bf16[192,256]{1,0:T(8,128)(2,1)S(1)}, u32[]{:S(2)}, u32[]{:S(2)}) %collective-permute-start.7) | collective-permute-done | bytes 98336 | tf_op jit(solution)/shard_map/ppermute | solution.py:285
  36.8 1.3 %collective-permute-done.8.refs_3_ = bf16[192,256]{1,0:T(8,128)(2,1)S(1)} collective-permute-done((bf16[192,256]{1,0:T(8,128)(2,1)S(1)}, bf16[192,256]{1,0:T(8,128)(2,1)S(1)}, u32[]{:S(2)}, u32[]{:S(2)}) %collective-permute-start.8) | collective-permute-done | bytes 98336 | tf_op jit(solution)/shard_map/ppermute | solution.py:285
  38.1 3.0 %shard_map.51 = bf16[3,2,128,1024]{3,2,1,0:T(8,128)(2,1)} custom-call(s32[3]{0:T(128)S(1)} %copy-done.2, bf16[192,256]{1,0:T(8,128)(2,1)S(1)} %add_convert_fusion.refs_0_, bf16[192,256]{1,0:T(8,128)(2,1)S(1)} %collective-permute-done.6.refs_1_, bf16[192,256]{1,0:T(8,128)(2,1)S(1)} %collective-permute-done.7.refs_2_, ...), custom_call_target="tpu_custom_call" | custom-call | flops 2400000000 | bytes 3000000 | tf_op jit(solution)/shard_map/pallas_call | solution.py:265
  (12 shorter events, 0.1 us)
Async XLA Ops:
  1.2 12.7 %collective-permute-start = (bf16[696,256]{1,0:T(8,128)(2,1)S(1)}, bf16[696,256]{1,0:T(8,128)(2,1)S(1)}, u32[]{:S(2)}, u32[]{:S(2)}) collective-permute-start(bf16[696,256]{1,0:T(8,128)(2,1)S(1)} %get-tuple-element.14.own_ref), channel_id=1, source_target_pairs={{4,0},{14,2},{8,4},{2,6},{12,8},{6,10},{0,12},{10,14},{5,1},{15,3}... | collective-permute-start | bytes 1069064 | tf_op jit(solution)/shard_map/ppermute | solution.py:327
  6.4 9.8 %collective-permute-start.1 = (bf16[696,256]{1,0:T(8,128)(2,1)S(1)}, bf16[696,256]{1,0:T(8,128)(2,1)S(1)}, u32[]{:S(2)}, u32[]{:S(2)}) collective-permute-start(bf16[696,256]{1,0:T(8,128)(2,1)S(1)} %get-tuple-element.15), channel_id=1, source_target_pairs={{0,2},{2,0},{4,6},{6,4},{8,10},{10,8},{12,14},{14,12},{1,3},{3,1},... | collective-permute-start | bytes 1069064 | tf_op jit(solution)/shard_map/ppermute | solution.py:326
  6.4 1.1 %copy-start = (bf16[1,2,256,3,216]{2,4,3,1,0:T(8,128)(2,1)S(1)}, bf16[1,2,256,3,216]{2,4,3,1,0:T(8,128)(2,1)}, u32[]{:S(2)}) copy-start(bf16[1,2,256,3,216]{2,4,3,1,0:T(8,128)(2,1)} %param.4) | copy-start | bytes 1990660
  7.5 0.7 %copy-start.1 = (bf16[1,3,3,3,2,216]{5,4,3,2,1,0:T(2,128)(2,1)S(1)}, bf16[1,3,3,3,2,216]{5,4,3,2,1,0:T(2,128)(2,1)}, u32[]{:S(2)}) copy-start(bf16[1,3,3,3,2,216]{5,4,3,2,1,0:T(2,128)(2,1)} %param.5) | copy-start | bytes 69988
  11.4 9.5 %copy-start.3 = (bf16[1,2,128,1024]{3,2,1,0:T(8,128)(2,1)S(1)}, bf16[1,2,128,1024]{3,2,1,0:T(8,128)(2,1)}, u32[]{:S(2)}) copy-start(bf16[1,2,128,1024]{3,2,1,0:T(8,128)(2,1)} %param.7) | copy-start | bytes 1572868
  17.4 20.7 %copy-start.2 = (s32[3]{0:T(128)S(1)}, s32[3]{0:T(128)}, u32[]{:S(2)}) copy-start(s32[3]{0:T(128)} %dirs_ref.1) | copy-start | bytes 40
  17.4 5.6 %collective-permute-start.2 = (bf16[192,256]{1,0:T(8,128)(2,1)S(1)}, bf16[192,256]{1,0:T(8,128)(2,1)S(1)}, u32[]{:S(2)}, u32[]{:S(2)}) collective-permute-start(bf16[192,256]{1,0:T(8,128)(2,1)S(1)} %get-tuple-element.17), channel_id=1, source_target_pairs={{0,6},{2,4},{4,2},{6,0},{8,14},{10,12},{12,10},{14,8},{1,7},{3,5},... | collective-permute-start | bytes 294920 | tf_op jit(solution)/shard_map/ppermute | solution.py:285
  17.9 5.4 %collective-permute-start.3 = (bf16[192,256]{1,0:T(8,128)(2,1)S(1)}, bf16[192,256]{1,0:T(8,128)(2,1)S(1)}, u32[]{:S(2)}, u32[]{:S(2)}) collective-permute-start(bf16[192,256]{1,0:T(8,128)(2,1)S(1)} %get-tuple-element.18), channel_id=1, source_target_pairs={{0,4},{2,6},{4,0},{6,2},{8,12},{10,14},{12,8},{14,10},{1,5},{3,7},... | collective-permute-start | bytes 294920 | tf_op jit(solution)/shard_map/ppermute | solution.py:285
  19.5 4.6 %collective-permute-start.4 = (bf16[192,256]{1,0:T(8,128)(2,1)S(1)}, bf16[192,256]{1,0:T(8,128)(2,1)S(1)}, u32[]{:S(2)}, u32[]{:S(2)}) collective-permute-start(bf16[192,256]{1,0:T(8,128)(2,1)S(1)} %get-tuple-element.19), channel_id=1, source_target_pairs={{0,2},{2,0},{4,6},{6,4},{8,10},{10,8},{12,14},{14,12},{1,3},{3,1},... | collective-permute-start | bytes 294920 | tf_op jit(solution)/shard_map/ppermute | solution.py:285
  20.9 13.5 %collective-permute-start.9 = (bf16[2,128,1024]{2,1,0:T(8,128)(2,1)S(1)}, bf16[2,128,1024]{2,1,0:T(8,128)(2,1)S(1)}, u32[]{:S(2)}, u32[]{:S(2)}) collective-permute-start(bf16[2,128,1024]{2,1,0:T(8,128)(2,1)S(1)} %bitcast.12), channel_id=1, source_target_pairs={{1,0},{0,1},{3,2},{2,3},{5,4},{4,5},{7,6},{6,7},{9,8},{8,9},{11,10... | collective-permute-start | bytes 1572872 | tf_op jit(solution)/shard_map/ppermute | solution.py:332
  24.2 6.6 %collective-permute-start.5 = (bf16[192,256]{1,0:T(8,128)(2,1)S(1)}, bf16[192,256]{1,0:T(8,128)(2,1)S(1)}, u32[]{:S(2)}, u32[]{:S(2)}) collective-permute-start(bf16[192,256]{1,0:T(8,128)(2,1)S(1)} %fusion), channel_id=1, source_target_pairs={{0,8},{2,10},{4,12},{6,14},{8,0},{10,2},{12,4},{14,6},{1,9},{3,11}... | collective-permute-start | bytes 294920 | tf_op jit(solution)/shard_map/ppermute | solution.py:285
  30.9 4.7 %collective-permute-start.6 = (bf16[192,256]{1,0:T(8,128)(2,1)S(1)}, bf16[192,256]{1,0:T(8,128)(2,1)S(1)}, u32[]{:S(2)}, u32[]{:S(2)}) collective-permute-start(bf16[192,256]{1,0:T(8,128)(2,1)S(1)} %add_convert_fusion.refs_0_), channel_id=1, source_target_pairs={{0,2},{2,0},{4,6},{6,4},{8,10},{10,8},{12,14},{14,12},{1,3},{3,1},... | collective-permute-start | bytes 294920 | tf_op jit(solution)/shard_map/ppermute | solution.py:285
  32.2 4.6 %collective-permute-start.7 = (bf16[192,256]{1,0:T(8,128)(2,1)S(1)}, bf16[192,256]{1,0:T(8,128)(2,1)S(1)}, u32[]{:S(2)}, u32[]{:S(2)}) collective-permute-start(bf16[192,256]{1,0:T(8,128)(2,1)S(1)} %add_convert_fusion.refs_0_), channel_id=1, source_target_pairs={{0,4},{2,6},{4,0},{6,2},{8,12},{10,14},{12,8},{14,10},{1,5},{3,7},... | collective-permute-start | bytes 294920 | tf_op jit(solution)/shard_map/ppermute | solution.py:285
  32.2 5.9 %collective-permute-start.8 = (bf16[192,256]{1,0:T(8,128)(2,1)S(1)}, bf16[192,256]{1,0:T(8,128)(2,1)S(1)}, u32[]{:S(2)}, u32[]{:S(2)}) collective-permute-start(bf16[192,256]{1,0:T(8,128)(2,1)S(1)} %add_convert_fusion.refs_0_), channel_id=1, source_target_pairs={{0,6},{2,4},{4,2},{6,0},{8,14},{10,12},{12,10},{14,8},{1,7},{3,5},... | collective-permute-start | bytes 294920 | tf_op jit(solution)/shard_map/ppermute | solution.py:285
